TPU v7x, 32 devices: a whole 2x2x4 slice. The times are simulated.
32 devices in a mesh: row: 4 (over z), col: 8 (over y, x, core).
Axes of the slice: x: 2, y: 2, z: 4, core: 2. Of those that a mesh axis runs over, the one named last changes fastest.
Arguments:
- features: bfloat16 [8, 1024, 256], P('col', 'row'), may hold values from -6 to 6
- weight: bfloat16 [256, 256], replicated, may hold values from -0.375 to 0.375
- cotangent: bfloat16 [8192, 256], P(('row', 'col')), may hold values from -6 to 6
- blk_vals: bfloat16 [4, 8, 192, 128, 128], P('row', 'col'), may hold values from -0.0546875 to 0.0546875
- blk_rows: int32 [4, 8, 192], P('row', 'col'), may hold values from 0 to 15
- blk_cols: int32 [4, 8, 192], P('row', 'col'), may hold values from 0 to 7
- blk_count: int32 [4, 8], P('row', 'col'), may hold values from 24 to 192, as said below
Outputs:
- activated: bfloat16 [8192, 256], P(('row', 'col'))
- grad_weight: float32 [256, 256], replicated
- grad_features: bfloat16 [8, 1024, 256], P('col', 'row')
Inputs may be any that keep to these rules, and one draw needn't show every extreme that they name: Only the first blk_count slots of a panel pair are used; a pair whose row and column node ranges intersect uses all 192, every other pair at most 96.
All inputs are finite; a program needn't handle non-finite values.
Results may differ from a plain program's by a relative error of at most 0.0059.
Values may be sent and summed in bfloat16 or wider, within the bound.
A program may use at most 128 MiB of HBM per device.

v0:
```python
import jax
import jax.numpy as jnp
from jax import lax
from jax.sharding import PartitionSpec as P


def block_terms(values, index, source, live_count, transpose):
    total_slots = values.shape[0]
    group = 64
    width = source.shape[-1]
    side = values.shape[-1]
    if transpose:
        form = "bji,bjf->bif"
    else:
        form = "bij,bjf->bif"

    def one_group(group_index, buffer):
        first = group_index * group
        block_vals = lax.dynamic_slice_in_dim(values, first, group, 0)
        block_ids = lax.dynamic_slice_in_dim(index, first, group, 0)
        picked = jnp.take(source, block_ids, axis=0)
        product = jnp.einsum(form, block_vals, picked, preferred_element_type=jnp.float32)
        alive = first + jnp.arange(group, dtype=jnp.int32) < live_count
        product = jnp.where(alive[:, None, None], product, 0.0)
        return lax.dynamic_update_slice_in_dim(buffer, product, first, 0)

    buffer = jnp.zeros((total_slots, side, width), jnp.float32)
    groups = total_slots // group
    return lax.fori_loop(0, groups, one_group, buffer)


def per_device(features, weight, cotangent, blk_vals, blk_rows, blk_cols, blk_count):
    rows_here = cotangent.shape[0]
    width = cotangent.shape[1]
    side = blk_vals.shape[-1]
    row_blocks = rows_here * lax.axis_size("col") // side
    col_blocks = rows_here * lax.axis_size("row") // side
    values = blk_vals[0, 0]
    row_ids = blk_rows[0, 0]
    col_ids = blk_cols[0, 0]
    live_count = blk_count[0, 0]
    panel = lax.all_gather(features, "row", axis=1, tiled=True)
    source = panel.reshape(col_blocks, side, width)
    products = block_terms(values, col_ids, source, live_count, False)
    partial_rows = jax.ops.segment_sum(products, row_ids, num_segments=row_blocks)
    own_rows = lax.psum_scatter(
        partial_rows.reshape(row_blocks * side, width), "col", scatter_dimension=0, tiled=True
    )
    aggregated = own_rows.astype(jnp.bfloat16)
    pre = jnp.dot(aggregated, weight, preferred_element_type=jnp.float32)
    sigma = jax.nn.sigmoid(pre)
    activated = (pre * sigma).astype(jnp.bfloat16)
    grad_pre = (cotangent.astype(jnp.float32) * sigma * (1.0 + pre * (1.0 - sigma))).astype(
        jnp.bfloat16
    )
    local_weight = lax.dot_general(
        aggregated, grad_pre, (((0,), (0,)), ((), ())), preferred_element_type=jnp.float32
    )
    grad_weight = lax.psum(local_weight, ("row", "col"))
    grad_agg = lax.dot_general(
        grad_pre, weight, (((1,), (1,)), ((), ())), preferred_element_type=jnp.float32
    ).astype(jnp.bfloat16)
    grad_rows = lax.all_gather(grad_agg, "col", axis=0, tiled=True)
    grad_source = grad_rows.reshape(row_blocks, side, width)
    back_products = block_terms(values, row_ids, grad_source, live_count, True)
    partial_cols = jax.ops.segment_sum(back_products, col_ids, num_segments=col_blocks)
    own_cols = lax.psum_scatter(
        partial_cols.reshape(col_blocks * side, width), "row", scatter_dimension=0, tiled=True
    )
    grad_features = own_cols.astype(jnp.bfloat16).reshape(1, rows_here, width)
    return (activated, grad_weight, grad_features)


def solution(mesh):
    return jax.shard_map(
        per_device,
        mesh=mesh,
        in_specs=(
            P("col", "row", None),
            P(),
            P(("row", "col"), None),
            P("row", "col", None, None, None),
            P("row", "col", None),
            P("row", "col", None),
            P("row", "col"),
        ),
        out_specs=(P(("row", "col"), None), P(), P("col", "row", None)),
        check_vma=False,
    )
```

profile of v0, /device:TPU:0, one launch (start us, length us, event | category | flops | bytes accessed | tf_op | source)
XLA Modules:
  0.0 423.9 jit_solution(15833494370647342353)
XLA Ops:
  7.2 17.6 %all_gather.6 = bf16[1,1024,256]{2,1,0:T(8,128)(2,1)S(1)} all-gather(bf16[1,256,256]{2,1,0:T(8,128)(2,1)} %param.11), channel_id=1, replica_groups=mesh['row'=4,'col'=8] {'row'}, dimensions={1}, use_global_device_ids=true | all-gather | bytes 655360 | tf_op jit(solution)/shard_map/all_gather | solution.py:42
  24.8 11.5 %broadcast.44.clone = f32[192,128,256]{2,1,0:T(8,128)} broadcast(f32[]{:T(128)} %constant.131.clone.1), dimensions={} | broadcast | bytes 25165828 | tf_op jit(solution)/shard_map/broadcast.3
  36.3 32.7 %while.26 = (s32[]{:T(128)}, f32[192,128,256]{2,1,0:T(8,128)}, s32[]{:T(128)}, bf16[192,128,128]{2,1,0:T(8,128)(2,1)}, s32[192]{0:T(256)S(1)}, /*index=5*/bf16[8...) while((s32[]{:T(128)}, f32[192,128,256]{2,1,0:T(8,128)}, s32[]{:T(128)}, ...), condition=%wide.region_1.0_spmd, body=%wide.region_0.1_spmd.sunk | while | flops 541066752 | bytes 23075232 | solution.py:29
  36.3 0.7 compare_and_fusion.4
  37.1 2.8 gather_fusion
  39.8 7.4 %select_dynamic-update-slice_fusion.4 = f32[192,128,256]{2,1,0:T(8,128)} fusion(f32[192,128,256]{2,1,0:T(8,128)} %get-tuple-element.358, s32[]{:T(128)S(6)} %select_n.88, pred[64]{0:T(512)(128)(4,1)S(1)} %get-tuple-element.335, bf16[64,128,256]{2,1,0:T(8,128)(2,1)} %gather_fusion, pred[64]{0:T(512)(128)(4,1)S(1)} %get-tuple-element.337, ...), kind=kOutput, calls=%fused_computation.4.clone.1 | convolution fusion | flops 541065216 | bytes 14681216 | tf_op jit(solution)/shard_map/while/body/eval_jaxpr/bij,bjf->bif/dot_general | solution.py:22
  47.9 2.8 gather_fusion
  50.7 7.4 %select_dynamic-update-slice_fusion.4 = f32[192,128,256]{2,1,0:T(8,128)} fusion(f32[192,128,256]{2,1,0:T(8,128)} %get-tuple-element.358, s32[]{:T(128)S(6)} %select_n.88, pred[64]{0:T(512)(128)(4,1)S(1)} %get-tuple-element.335, bf16[64,128,256]{2,1,0:T(8,128)(2,1)} %gather_fusion, pred[64]{0:T(512)(128)(4,1)S(1)} %get-tuple-element.337, ...), kind=kOutput, calls=%fused_computation.4.clone.1 | convolution fusion | flops 541065216 | bytes 14681216 | tf_op jit(solution)/shard_map/while/body/eval_jaxpr/bij,bjf->bif/dot_general | solution.py:22
  58.8 2.8 gather_fusion
  61.6 7.4 %select_dynamic-update-slice_fusion.4 = f32[192,128,256]{2,1,0:T(8,128)} fusion(f32[192,128,256]{2,1,0:T(8,128)} %get-tuple-element.358, s32[]{:T(128)S(6)} %select_n.88, pred[64]{0:T(512)(128)(4,1)S(1)} %get-tuple-element.335, bf16[64,128,256]{2,1,0:T(8,128)(2,1)} %gather_fusion, pred[64]{0:T(512)(128)(4,1)S(1)} %get-tuple-element.337, ...), kind=kOutput, calls=%fused_computation.4.clone.1 | convolution fusion | flops 541065216 | bytes 14681216 | tf_op jit(solution)/shard_map/while/body/eval_jaxpr/bij,bjf->bif/dot_general | solution.py:22
  69.2 36.1 %scatter_fusion = f32[16,128,256]{2,1,0:T(8,128)S(1)} fusion(f32[16,128,256]{2,1,0:T(8,128)S(1)} %broadcast_in_dim.108, s32[192]{0:T(256)S(1)} %bitcast.22, f32[192,128,256]{2,1,0:T(8,128)} %get-tuple-element.221), kind=kCustom, calls=%fused_computation.2 | custom fusion | flops 6291456 | bytes 75498240 | tf_op jit(solution)/shard_map/scatter-add | solution.py:45
  105.3 1.3 copy-done.4
  106.7 43.0 %reduce-scatter.3.cloned.1.call-done = f32[256,256]{1,0:T(8,128)} async-done(((f32[2048,256]{1,0:T(8,128)}), f32[256,256]{1,0:T(8,128)}) %reduce-scatter.3.cloned.1.call-update) | async-done | bytes 262160 | tf_op jit(solution)/shard_map/reduce_scatter | solution.py:46
  149.6 1.9 multiply_convert_fusion
  151.5 0.9 convolution_convert_fusion
  152.5 8.6 %copy.10 = bf16[1,1,192,128,128]{3,4,2,1,0:T(8,128)(2,1)} copy(bf16[1,1,192,128,128]{4,3,2,1,0:T(8,128)(2,1)} %bitcast.20) | data formatting | bytes 12582912 | tf_op args[3]
  161.0 14.9 %all-gather.2.cloned.1.call-done = bf16[2048,256]{1,0:T(8,128)(2,1)} async-done(((bf16[256,256]{1,0:T(8,128)(2,1)}), bf16[2048,256]{1,0:T(8,128)(2,1)}) %all-gather.2.cloned.1.call-update) | async-done | bytes 1048592 | tf_op jit(solution)/shard_map/all_gather | solution.py:63
  176.0 11.5 %broadcast.44 = f32[192,128,256]{2,1,0:T(8,128)} broadcast(f32[]{:T(128)} %constant.131.clone.1), dimensions={} | broadcast | bytes 25165828 | tf_op jit(solution)/shard_map/broadcast.3
  187.4 32.7 %while.27 = (s32[]{:T(128)}, f32[192,128,256]{2,1,0:T(8,128)}, s32[]{:T(128)}, bf16[192,128,128]{1,2,0:T(8,128)(2,1)}, s32[192]{0:T(256)S(1)}, /*index=5*/bf16[1...) while((s32[]{:T(128)}, f32[192,128,256]{2,1,0:T(8,128)}, s32[]{:T(128)}, ...), condition=%wide.region_6.7_spmd, body=%wide.region_5.6_spmd.sunk | while | flops 541066752 | bytes 23075232 | solution.py:29
  188.2 2.8 gather_fusion.1
  191.0 7.4 %select_dynamic-update-slice_fusion.5 = f32[192,128,256]{2,1,0:T(8,128)} fusion(f32[192,128,256]{2,1,0:T(8,128)} %get-tuple-element.388, s32[]{:T(128)S(6)} %select_n.91, pred[64]{0:T(512)(128)(4,1)S(1)} %get-tuple-element.344, bf16[64,128,256]{2,1,0:T(8,128)(2,1)} %gather_fusion.1, pred[64]{0:T(512)(128)(4,1)S(1)} %get-tuple-element.346, ...), kind=kOutput, calls=%fused_computation.16.clone.1 | convolution fusion | flops 541065216 | bytes 14681216 | tf_op jit(solution)/shard_map/while/body/eval_jaxpr/bji,bjf->bif/dot_general | solution.py:22
  199.1 2.8 gather_fusion.1
  201.8 7.4 %select_dynamic-update-slice_fusion.5 = f32[192,128,256]{2,1,0:T(8,128)} fusion(f32[192,128,256]{2,1,0:T(8,128)} %get-tuple-element.388, s32[]{:T(128)S(6)} %select_n.91, pred[64]{0:T(512)(128)(4,1)S(1)} %get-tuple-element.344, bf16[64,128,256]{2,1,0:T(8,128)(2,1)} %gather_fusion.1, pred[64]{0:T(512)(128)(4,1)S(1)} %get-tuple-element.346, ...), kind=kOutput, calls=%fused_computation.16.clone.1 | convolution fusion | flops 541065216 | bytes 14681216 | tf_op jit(solution)/shard_map/while/body/eval_jaxpr/bji,bjf->bif/dot_general | solution.py:22
  210.0 2.8 gather_fusion.1
  212.7 7.4 %select_dynamic-update-slice_fusion.5 = f32[192,128,256]{2,1,0:T(8,128)} fusion(f32[192,128,256]{2,1,0:T(8,128)} %get-tuple-element.388, s32[]{:T(128)S(6)} %select_n.91, pred[64]{0:T(512)(128)(4,1)S(1)} %get-tuple-element.344, bf16[64,128,256]{2,1,0:T(8,128)(2,1)} %gather_fusion.1, pred[64]{0:T(512)(128)(4,1)S(1)} %get-tuple-element.346, ...), kind=kOutput, calls=%fused_computation.16.clone.1 | convolution fusion | flops 541065216 | bytes 14681216 | tf_op jit(solution)/shard_map/while/body/eval_jaxpr/bji,bjf->bif/dot_general | solution.py:22
  220.2 36.0 %scatter_fusion.1 = f32[8,128,256]{2,1,0:T(8,128)S(1)} fusion(f32[8,128,256]{2,1,0:T(8,128)S(1)} %broadcast_in_dim.109, s32[192]{0:T(256)S(1)} %get-tuple-element.427, f32[192,128,256]{2,1,0:T(8,128)} %get-tuple-element.222), kind=kCustom, calls=%fused_computation.3 | custom fusion | flops 6291456 | bytes 75498240 | tf_op jit(solution)/shard_map/scatter-add | solution.py:66
  256.2 1.0 copy-done.2
  257.3 0.9 fusion.18
  258.2 26.4 %reduce-scatter.5.cloned.1.call-done = f32[256,256]{1,0:T(8,128)} async-done(((f32[1024,256]{1,0:T(8,128)}), f32[256,256]{1,0:T(8,128)}) %reduce-scatter.5.cloned.1.call-update) | async-done | bytes 262160 | tf_op jit(solution)/shard_map/reduce_scatter | solution.py:67
  284.7 1.6 convert_bitcast_fusion
  286.3 129.4 %all-reduce.2.cloned.1.call-done = f32[256,256]{1,0:T(8,128)} async-done(((f32[256,256]{1,0:T(8,128)}), f32[256,256]{1,0:T(8,128)}) %all-reduce.2.cloned.1.call-update) | async-done | bytes 262160 | tf_op jit(solution)/shard_map/psum | solution.py:59
  415.7 1.7 copy.30
  (37 shorter events, 4.2 us)
Async XLA Ops:
  7.2 142.5 %copy-start = (bf16[256,256]{1,0:T(8,128)(2,1)S(1)}, bf16[256,256]{1,0:T(8,128)(2,1)}, u32[]{:S(2)}) copy-start(bf16[256,256]{1,0:T(8,128)(2,1)} %param.12) | copy-start | bytes 393220
  7.2 142.5 %reduce-scatter.3.cloned.1.call-start = ((), (), s32[]{:S(2)}) async-start(), calls=%async_computation.2 | async-start | bytes 2359296 | tf_op jit(solution)/shard_map/reduce_scatter | solution.py:46
  24.8 11.5 %copy-start.7 = (s32[1,1,192]{2,1,0:T(1,128)S(1)}, s32[1,1,192]{2,1,0:T(1,128)}, u32[]{:S(2)}) copy-start(s32[1,1,192]{2,1,0:T(1,128)} %param.16) | copy-start | bytes 2308
  36.3 32.9 %copy-start.6 = (s32[1,1,192]{2,1,0:T(1,128)S(1)}, s32[1,1,192]{2,1,0:T(1,128)}, u32[]{:S(2)}) copy-start(s32[1,1,192]{2,1,0:T(1,128)} %param.15) | copy-start | bytes 2308
  69.2 80.4 %copy-start.8 = (bf16[256,256]{1,0:T(8,128)(2,1)S(1)}, bf16[256,256]{1,0:T(8,128)(2,1)}, u32[]{:S(2)}) copy-start(bf16[256,256]{1,0:T(8,128)(2,1)} %param.13) | copy-start | bytes 393220
  105.3 1.3 copy-start.4
  106.6 69.3 %all-gather.2.cloned.1.call-start = ((), (), s32[]{:S(2)}) async-start(), calls=%async_computation.4 | async-start | bytes 1179648 | tf_op jit(solution)/shard_map/all_gather | solution.py:63
  152.4 132.2 %reduce-scatter.5.cloned.1.call-start = ((), (), s32[]{:S(2)}) async-start(), calls=%async_computation.5 | async-start | bytes 1310720 | tf_op jit(solution)/shard_map/reduce_scatter | solution.py:67
  176.0 11.5 %copy-start.3 = (bf16[2048,256]{1,0:T(8,128)(2,1)S(1)}, bf16[2048,256]{1,0:T(8,128)(2,1)}, u32[]{:S(2)}) copy-start(bf16[2048,256]{1,0:T(8,128)(2,1)} %all-gather.2.cloned.1.call-done) | copy-start | bytes 3145732
  220.2 37.1 %copy-start.5 = (f32[256,256]{1,0:T(8,128)S(1)}, f32[256,256]{1,0:T(8,128)}, u32[]{:S(2)}) copy-start(f32[256,256]{1,0:T(8,128)} %reduce-scatter.3.cloned.1.call-done) | copy-start | bytes 786436
  220.2 197.1 %copy-start.1 = (bf16[256,256]{1,0:T(8,128)(2,1)S(1)}, bf16[256,256]{1,0:T(8,128)(2,1)}, u32[]{:S(2)}) copy-start(bf16[256,256]{1,0:T(8,128)(2,1)} %param.12) | copy-start | bytes 393220
  256.2 1.0 copy-start.2
  257.2 158.5 %all-reduce.2.cloned.1.call-start = ((), (), s32[]{:S(2)}) async-start(), calls=%async_computation.3 | async-start | bytes 524288 | tf_op jit(solution)/shard_map/psum | solution.py:59
Sparse Core Ops, SparseCore 0:
  106.7 42.8 reduce-scatter.2
  152.6 23.3 all-gather.1
  257.3 27.2 reduce-scatter.4
  290.6 125.0 all-reduce.1
where the time goes:
time: 425 us; the launch traced here: 424 us
  waiting for transfers between devices  214 us (50%)
  other arithmetic  78.1 us (18%)
  local copies, waits for them, and re-layouts  52.5 us (12%)
  matrix products  47.9 us (11%)
  blocking collectives  17.6 us (4%)
  between operations  13.9 us (3%)
    psum x1, waiting for transfers between devices, per_device(): grad_weight = lax.psum(local_weight, ('row', 'col'))  129 us
    dot_general x6, matrix products, one_group(): jnp.einsum(form, block_vals, picked, preferred_element_type=jnp.float32)  44.3 us
    reduce_scatter x1, waiting for transfers between devices, per_device(): lax.psum_scatter(partial_rows.reshape(row_blocks * side, width), 'col', s...  43 us
    scatter-add x1, other arithmetic, per_device(): jax.ops.segment_sum(products, row_ids, num_segments=row_blocks)  36.1 us
    scatter-add x1, other arithmetic, per_device(): jax.ops.segment_sum(back_products, col_ids, num_segments=col_blocks)  36 us
    reduce_scatter x1, waiting for transfers between devices, per_device(): lax.psum_scatter(partial_cols.reshape(col_blocks * side, width), 'row', s...  26.4 us
    another operation x2, local copies, waits for them, and re-layouts  23 us
    all_gather x1, blocking collectives, per_device(): panel = lax.all_gather(features, 'row', axis=1, tiled=True)  17.6 us
  transfers between devices with their start and end apart: 4, of which 4 were waited for; matrix products, arithmetic and copies ran while one was open for 3% of the time, Pallas kernels for 0%

commit v1 on v0

--- a/solution.py
+++ b/solution.py
@@ -2,6 +2,12 @@
 import jax.numpy as jnp
 from jax import lax
 from jax.sharding import PartitionSpec as P
+
+
+def slots_direct(raw, device_axis, lane_axis):
+    local_next = lax.psum(raw, device_axis)
+    main = lax.psum(local_next, lane_axis)
+    return main
 
 
 def block_terms(values, index, source, live_count, transpose):
@@ -56,7 +62,7 @@
     local_weight = lax.dot_general(
         aggregated, grad_pre, (((0,), (0,)), ((), ())), preferred_element_type=jnp.float32
     )
-    grad_weight = lax.psum(local_weight, ("row", "col"))
+    grad_weight = slots_direct(local_weight, "col", "row")
     grad_agg = lax.dot_general(
         grad_pre, weight, (((1,), (1,)), ((), ())), preferred_element_type=jnp.float32
     ).astype(jnp.bfloat16)

time: 425 us -> 331 us (0.78)
  waiting for transfers between devices: 214 us -> 119 us
    psum x1 -> x2, waiting for transfers between devices: 129 us -> 34.7 us  [the longest x1 34.7 us: slots_direct(): main = lax.psum(local_next, lane_axis)]
  transfers between devices with their start and end apart: 4 -> 5, of which waited for: 4 -> 4; matrix products, arithmetic and copies ran while one was open for 3% -> 28% of each run, Pallas kernels for 0% -> 0%
where the time goes in v1:
time: 331 us; the launch traced here: 329 us
  waiting for transfers between devices  119 us (36%)
  other arithmetic  78.1 us (24%)
  local copies, waits for them, and re-layouts  52.6 us (16%)
  matrix products  48 us (15%)
  blocking collectives  17.6 us (5%)
  between operations  13.9 us (4%)
    dot_general x6, matrix products, one_group(): jnp.einsum(form, block_vals, picked, preferred_element_type=jnp.float32)  44.3 us
    reduce_scatter x1, waiting for transfers between devices, per_device(): lax.psum_scatter(partial_rows.reshape(row_blocks * side, width), 'col', s...  43 us
    scatter-add x1, other arithmetic, per_device(): jax.ops.segment_sum(products, row_ids, num_segments=row_blocks)  36.1 us
    scatter-add x1, other arithmetic, per_device(): jax.ops.segment_sum(back_products, col_ids, num_segments=col_blocks)  36 us
    psum x1, waiting for transfers between devices, slots_direct(): main = lax.psum(local_next, lane_axis)  34.7 us
    reduce_scatter x1, waiting for transfers between devices, per_device(): lax.psum_scatter(partial_cols.reshape(col_blocks * side, width), 'row', s...  26.9 us
    another operation x2, local copies, waits for them, and re-layouts  23 us
    all_gather x1, blocking collectives, per_device(): panel = lax.all_gather(features, 'row', axis=1, tiled=True)  17.6 us
  transfers between devices with their start and end apart: 5, of which 4 were waited for; matrix products, arithmetic and copies ran while one was open for 28% of the time, Pallas kernels for 0%

profile of v1, /device:TPU:0, one launch (start us, length us, event | category | flops | bytes accessed | tf_op | source)
XLA Modules:
  0.0 329.3 jit_solution(2362421956407925268)
XLA Ops:
  7.2 17.6 %all_gather.6 = bf16[1,1024,256]{2,1,0:T(8,128)(2,1)S(1)} all-gather(bf16[1,256,256]{2,1,0:T(8,128)(2,1)} %param.11), channel_id=1, replica_groups=mesh['row'=4,'col'=8] {'row'}, dimensions={1}, use_global_device_ids=true | all-gather | bytes 655360 | tf_op jit(solution)/shard_map/all_gather | solution.py:48
  24.8 11.5 %broadcast.44.clone = f32[192,128,256]{2,1,0:T(8,128)} broadcast(f32[]{:T(128)} %constant.131.clone.1), dimensions={} | broadcast | bytes 25165828 | tf_op jit(solution)/shard_map/broadcast.3
  36.3 32.7 %while.26 = (s32[]{:T(128)}, f32[192,128,256]{2,1,0:T(8,128)}, s32[]{:T(128)}, bf16[192,128,128]{2,1,0:T(8,128)(2,1)}, s32[192]{0:T(256)S(1)}, /*index=5*/bf16[8...) while((s32[]{:T(128)}, f32[192,128,256]{2,1,0:T(8,128)}, s32[]{:T(128)}, ...), condition=%wide.region_1.0_spmd, body=%wide.region_0.1_spmd.sunk | while | flops 541066752 | bytes 23075232 | solution.py:35
  36.3 0.7 compare_and_fusion.4
  37.1 2.8 gather_fusion
  39.8 7.4 %select_dynamic-update-slice_fusion.4 = f32[192,128,256]{2,1,0:T(8,128)} fusion(f32[192,128,256]{2,1,0:T(8,128)} %get-tuple-element.358, s32[]{:T(128)S(6)} %select_n.88, pred[64]{0:T(512)(128)(4,1)S(1)} %get-tuple-element.335, bf16[64,128,256]{2,1,0:T(8,128)(2,1)} %gather_fusion, pred[64]{0:T(512)(128)(4,1)S(1)} %get-tuple-element.337, ...), kind=kOutput, calls=%fused_computation.4.clone.1 | convolution fusion | flops 541065216 | bytes 14681216 | tf_op jit(solution)/shard_map/while/body/eval_jaxpr/bij,bjf->bif/dot_general | solution.py:28
  47.9 2.8 gather_fusion
  50.7 7.4 %select_dynamic-update-slice_fusion.4 = f32[192,128,256]{2,1,0:T(8,128)} fusion(f32[192,128,256]{2,1,0:T(8,128)} %get-tuple-element.358, s32[]{:T(128)S(6)} %select_n.88, pred[64]{0:T(512)(128)(4,1)S(1)} %get-tuple-element.335, bf16[64,128,256]{2,1,0:T(8,128)(2,1)} %gather_fusion, pred[64]{0:T(512)(128)(4,1)S(1)} %get-tuple-element.337, ...), kind=kOutput, calls=%fused_computation.4.clone.1 | convolution fusion | flops 541065216 | bytes 14681216 | tf_op jit(solution)/shard_map/while/body/eval_jaxpr/bij,bjf->bif/dot_general | solution.py:28
  58.8 2.8 gather_fusion
  61.6 7.4 %select_dynamic-update-slice_fusion.4 = f32[192,128,256]{2,1,0:T(8,128)} fusion(f32[192,128,256]{2,1,0:T(8,128)} %get-tuple-element.358, s32[]{:T(128)S(6)} %select_n.88, pred[64]{0:T(512)(128)(4,1)S(1)} %get-tuple-element.335, bf16[64,128,256]{2,1,0:T(8,128)(2,1)} %gather_fusion, pred[64]{0:T(512)(128)(4,1)S(1)} %get-tuple-element.337, ...), kind=kOutput, calls=%fused_computation.4.clone.1 | convolution fusion | flops 541065216 | bytes 14681216 | tf_op jit(solution)/shard_map/while/body/eval_jaxpr/bij,bjf->bif/dot_general | solution.py:28
  69.2 36.1 %scatter_fusion = f32[16,128,256]{2,1,0:T(8,128)S(1)} fusion(f32[16,128,256]{2,1,0:T(8,128)S(1)} %broadcast_in_dim.108, s32[192]{0:T(256)S(1)} %bitcast.22, f32[192,128,256]{2,1,0:T(8,128)} %get-tuple-element.221), kind=kCustom, calls=%fused_computation.2 | custom fusion | flops 6291456 | bytes 75498240 | tf_op jit(solution)/shard_map/scatter-add | solution.py:51
  105.3 1.3 copy-done.4
  106.7 43.0 %reduce-scatter.3.cloned.1.call-done = f32[256,256]{1,0:T(8,128)} async-done(((f32[2048,256]{1,0:T(8,128)}), f32[256,256]{1,0:T(8,128)}) %reduce-scatter.3.cloned.1.call-update) | async-done | bytes 262160 | tf_op jit(solution)/shard_map/reduce_scatter | solution.py:52
  149.6 1.9 multiply_convert_fusion
  151.5 0.9 convolution_convert_fusion
  152.5 8.6 %copy.10 = bf16[1,1,192,128,128]{3,4,2,1,0:T(8,128)(2,1)} copy(bf16[1,1,192,128,128]{4,3,2,1,0:T(8,128)(2,1)} %bitcast.20) | data formatting | bytes 12582912 | tf_op args[3]
  161.1 0.9 fusion.18
  162.1 13.9 %all-gather.2.cloned.1.call-done = bf16[2048,256]{1,0:T(8,128)(2,1)} async-done(((bf16[256,256]{1,0:T(8,128)(2,1)}), bf16[2048,256]{1,0:T(8,128)(2,1)}) %all-gather.2.cloned.1.call-update) | async-done | bytes 1048592 | tf_op jit(solution)/shard_map/all_gather | solution.py:69
  176.0 11.6 %broadcast.44 = f32[192,128,256]{2,1,0:T(8,128)} broadcast(f32[]{:T(128)} %constant.131.clone.1), dimensions={} | broadcast | bytes 25165828 | tf_op jit(solution)/shard_map/broadcast.3
  187.5 32.7 %while.27 = (s32[]{:T(128)}, f32[192,128,256]{2,1,0:T(8,128)}, s32[]{:T(128)}, bf16[192,128,128]{1,2,0:T(8,128)(2,1)}, s32[192]{0:T(256)S(1)}, /*index=5*/bf16[1...) while((s32[]{:T(128)}, f32[192,128,256]{2,1,0:T(8,128)}, s32[]{:T(128)}, ...), condition=%wide.region_7.8_spmd, body=%wide.region_6.7_spmd.sunk | while | flops 541066752 | bytes 23075232 | solution.py:35
  188.2 2.8 gather_fusion.1
  191.0 7.4 %select_dynamic-update-slice_fusion.5 = f32[192,128,256]{2,1,0:T(8,128)} fusion(f32[192,128,256]{2,1,0:T(8,128)} %get-tuple-element.388, s32[]{:T(128)S(6)} %select_n.91, pred[64]{0:T(512)(128)(4,1)S(1)} %get-tuple-element.344, bf16[64,128,256]{2,1,0:T(8,128)(2,1)} %gather_fusion.1, pred[64]{0:T(512)(128)(4,1)S(1)} %get-tuple-element.346, ...), kind=kOutput, calls=%fused_computation.16.clone.1 | convolution fusion | flops 541065216 | bytes 14681216 | tf_op jit(solution)/shard_map/while/body/eval_jaxpr/bji,bjf->bif/dot_general | solution.py:28
  199.1 2.8 gather_fusion.1
  201.9 7.4 %select_dynamic-update-slice_fusion.5 = f32[192,128,256]{2,1,0:T(8,128)} fusion(f32[192,128,256]{2,1,0:T(8,128)} %get-tuple-element.388, s32[]{:T(128)S(6)} %select_n.91, pred[64]{0:T(512)(128)(4,1)S(1)} %get-tuple-element.344, bf16[64,128,256]{2,1,0:T(8,128)(2,1)} %gather_fusion.1, pred[64]{0:T(512)(128)(4,1)S(1)} %get-tuple-element.346, ...), kind=kOutput, calls=%fused_computation.16.clone.1 | convolution fusion | flops 541065216 | bytes 14681216 | tf_op jit(solution)/shard_map/while/body/eval_jaxpr/bji,bjf->bif/dot_general | solution.py:28
  210.1 2.8 gather_fusion.1
  212.8 7.4 %select_dynamic-update-slice_fusion.5 = f32[192,128,256]{2,1,0:T(8,128)} fusion(f32[192,128,256]{2,1,0:T(8,128)} %get-tuple-element.388, s32[]{:T(128)S(6)} %select_n.91, pred[64]{0:T(512)(128)(4,1)S(1)} %get-tuple-element.344, bf16[64,128,256]{2,1,0:T(8,128)(2,1)} %gather_fusion.1, pred[64]{0:T(512)(128)(4,1)S(1)} %get-tuple-element.346, ...), kind=kOutput, calls=%fused_computation.16.clone.1 | convolution fusion | flops 541065216 | bytes 14681216 | tf_op jit(solution)/shard_map/while/body/eval_jaxpr/bji,bjf->bif/dot_general | solution.py:28
  220.3 36.0 %scatter_fusion.1 = f32[8,128,256]{2,1,0:T(8,128)S(1)} fusion(f32[8,128,256]{2,1,0:T(8,128)S(1)} %broadcast_in_dim.109, s32[192]{0:T(256)S(1)} %get-tuple-element.431, f32[192,128,256]{2,1,0:T(8,128)} %get-tuple-element.222), kind=kCustom, calls=%fused_computation.3 | custom fusion | flops 6291456 | bytes 75498240 | tf_op jit(solution)/shard_map/scatter-add | solution.py:72
  256.4 1.0 copy-done.2
  257.9 26.9 %reduce-scatter.5.cloned.1.call-done = f32[256,256]{1,0:T(8,128)} async-done(((f32[1024,256]{1,0:T(8,128)}), f32[256,256]{1,0:T(8,128)}) %reduce-scatter.5.cloned.1.call-update) | async-done | bytes 262160 | tf_op jit(solution)/shard_map/reduce_scatter | solution.py:73
  284.8 1.6 convert_bitcast_fusion
  286.4 34.7 %all-reduce.5.cloned.1.call-done = f32[256,256]{1,0:T(8,128)} async-done(((f32[256,256]{1,0:T(8,128)}), f32[256,256]{1,0:T(8,128)}) %all-reduce.5.cloned.1.call-update) | async-done | bytes 262160 | tf_op jit(solution)/shard_map/psum | solution.py:9
  321.1 1.7 copy.31
  (40 shorter events, 4.8 us)
Async XLA Ops:
  7.2 142.5 %copy-start = (bf16[256,256]{1,0:T(8,128)(2,1)S(1)}, bf16[256,256]{1,0:T(8,128)(2,1)}, u32[]{:S(2)}) copy-start(bf16[256,256]{1,0:T(8,128)(2,1)} %param.12) | copy-start | bytes 393220
  7.2 142.5 %reduce-scatter.3.cloned.1.call-start = ((), (), s32[]{:S(2)}) async-start(), calls=%async_computation.2 | async-start | bytes 2359296 | tf_op jit(solution)/shard_map/reduce_scatter | solution.py:52
  24.8 11.5 %copy-start.7 = (s32[1,1,192]{2,1,0:T(1,128)S(1)}, s32[1,1,192]{2,1,0:T(1,128)}, u32[]{:S(2)}) copy-start(s32[1,1,192]{2,1,0:T(1,128)} %param.16) | copy-start | bytes 2308
  36.3 32.9 %copy-start.6 = (s32[1,1,192]{2,1,0:T(1,128)S(1)}, s32[1,1,192]{2,1,0:T(1,128)}, u32[]{:S(2)}) copy-start(s32[1,1,192]{2,1,0:T(1,128)} %param.15) | copy-start | bytes 2308
  69.2 80.4 %copy-start.8 = (bf16[256,256]{1,0:T(8,128)(2,1)S(1)}, bf16[256,256]{1,0:T(8,128)(2,1)}, u32[]{:S(2)}) copy-start(bf16[256,256]{1,0:T(8,128)(2,1)} %param.13) | copy-start | bytes 393220
  105.3 1.3 copy-start.4
  106.6 69.3 %all-gather.2.cloned.1.call-start = ((), (), s32[]{:S(2)}) async-start(), calls=%async_computation.5 | async-start | bytes 1179648 | tf_op jit(solution)/shard_map/all_gather | solution.py:69
  152.4 8.7 %copy-start.5 = (f32[256,256]{1,0:T(8,128)S(1)}, f32[256,256]{1,0:T(8,128)}, u32[]{:S(2)}) copy-start(f32[256,256]{1,0:T(8,128)} %reduce-scatter.3.cloned.1.call-done) | copy-start | bytes 786436
  152.4 105.0 %all-reduce.3.cloned.1.call-start = ((), (), s32[]{:S(2)}) async-start(), calls=%async_computation.3 | async-start | bytes 524288 | tf_op jit(solution)/shard_map/psum | solution.py:8
  162.0 122.7 %reduce-scatter.5.cloned.1.call-start = ((), (), s32[]{:S(2)}) async-start(), calls=%async_computation.6 | async-start | bytes 1310720 | tf_op jit(solution)/shard_map/reduce_scatter | solution.py:73
  176.0 11.6 %copy-start.3 = (bf16[2048,256]{1,0:T(8,128)(2,1)S(1)}, bf16[2048,256]{1,0:T(8,128)(2,1)}, u32[]{:S(2)}) copy-start(bf16[2048,256]{1,0:T(8,128)(2,1)} %all-gather.2.cloned.1.call-done) | copy-start | bytes 3145732
  220.3 102.5 %copy-start.1 = (bf16[256,256]{1,0:T(8,128)(2,1)S(1)}, bf16[256,256]{1,0:T(8,128)(2,1)}, u32[]{:S(2)}) copy-start(bf16[256,256]{1,0:T(8,128)(2,1)} %param.12) | copy-start | bytes 393220
  256.3 1.0 copy-start.2
  257.3 63.7 %all-reduce.5.cloned.1.call-start = ((), (), s32[]{:S(2)}) async-start(), calls=%async_computation.4 | async-start | bytes 524288 | tf_op jit(solution)/shard_map/psum | solution.py:9
Sparse Core Ops, SparseCore 0:
  106.7 42.8 reduce-scatter.2
  152.6 23.3 all-gather.1
  179.6 53.8 all-reduce.2
  257.5 27.2 reduce-scatter.4
  287.0 34.0 all-reduce.4
